TPU v7x, 32 devices: a whole 2x2x4 slice. The times are simulated.
32 devices in a mesh: groups: 2 (over y), section: 4 (over x, core), lat: 4 (over z).
Axes of the slice: x: 2, y: 2, z: 4, core: 2. Of those that a mesh axis runs over, the one named last changes fastest.
Arguments:
- member_slabs: float32 [8, 16, 64, 768], P(('groups', 'section'), 'lat'), parts along dimension 0, may hold values from -6 to 6
- member_codes: int32 [2, 8], P(None, 'groups'), parts along dimension 1, may hold values from 0 to 31
- member_table: float32 [32, 768], replicated, may hold values from -4 to 4
- land_sea: int32 [16, 64], P('lat'), may hold values 0 or 1
- land_embed: float32 [4, 768], P('section'), may hold values from -4 to 4
- attention_gain: float32 [4, 768], P('section'), may hold values from 0.25 to 1.75
- project_in: bfloat16 [4, 768, 2304], P('section'), may hold values from -0.21875 to 0.21875
- logit_scale: float32 [4, 12], P('section'), may hold values from 3 to 25
- position_kernel: float32 [4, 5, 3, 768], P('section'), may hold values from -1.5 to 1.5
- project_out: bfloat16 [4, 768, 768], P('section'), may hold values from -0.21875 to 0.21875
- feed_gain: float32 [4, 768], P('section'), may hold values from 0.25 to 1.75
- expand_weight: bfloat16 [4, 768, 2048], P('section'), may hold values from -0.21875 to 0.21875
- reduce_weight: bfloat16 [4, 2048, 768], P('section'), may hold values from -0.125 to 0.125
- window_offset: int32 [4], P('section'), may hold values from 1 to 31
Outputs:
- updated_slabs: float32 [8, 16, 64, 768], P(('groups', 'section'), 'lat'), parts along dimension 0
There are 2 independent parts, one for each index of `groups`. A program takes and returns all parts, laid end to end along the dimension named above; an argument that names none is the same for every part. Nothing has to cross between parts.
Inputs may be any that keep to these rules, and one draw needn't show every extreme that they name: member_codes[t, m] names the perturbation embedding of member m at tick t. `land_sea`: 1 marks land.
All inputs are finite; a program needn't handle non-finite values. No bound on the sum of `land_sea` on one device may be relied on, other than what follows from the above.
Results may differ from a plain program's by a relative error of at most 0.0085.
Values may be sent and summed in bfloat16 or wider, within the bound.
A program may use at most 128 MiB of HBM per device.

v0:
```python
import functools
import math

import jax
import jax.numpy as jnp
from jax import lax
from jax.experimental import pallas as pl
from jax.experimental.pallas import tpu as pltpu
from jax.sharding import PartitionSpec as P

WIN_LAT = 4
WIN_LON = 32
TICKS = 2
EPSILON = 1e-06

F32 = jnp.float32
BF16 = jnp.bfloat16
LANES = 128
COLS = 256
MESH = pl.DeviceIdType.MESH


def norm_scale(values, gain_row):
    mean_square = jnp.mean(values * values, axis=-1, keepdims=True)
    return values * lax.rsqrt(mean_square + EPSILON) * gain_row


def dot(left, right):
    return jnp.dot(left, right, preferred_element_type=F32)


def head_unit(values, head_width):
    groups = []
    for start in range(0, values.shape[1], LANES):
        part = values[:, start : start + LANES]
        lane = lax.broadcasted_iota(jnp.int32, part.shape, 1)
        square = part * part
        factor = None
        for low in range(0, LANES, head_width):
            inside = (lane >= low) & (lane < low + head_width)
            total = jnp.sum(jnp.where(inside, square, 0.0), axis=-1, keepdims=True)
            scale = lax.rsqrt(total + EPSILON)
            factor = scale if factor is None else jnp.where(inside, scale, factor)
        groups.append((part * factor).astype(BF16))
    return jnp.concatenate(groups, axis=1)


def split_index(index, length, count):
    whole = jnp.zeros_like(index)
    for step in range(1, count):
        whole = whole + (index >= step * length).astype(jnp.int32)
    return whole, index - whole * length


def kernel(
    sizes,
    codes,
    offsets,
    head_scale,
    slab,
    table,
    land,
    land_embed,
    attention_gain,
    feed_gain,
    position_kernel,
    in_hbm,
    out_hbm,
    up_hbm,
    down_hbm,
    result,
    w_in,
    w_out,
    w_up,
    w_down,
    stream,
    mixed,
    normed,
    halo,
    queries,
    keys,
    values,
    blended,
    normed_mix,
    hidden,
    window,
    ring_out,
    ring_in,
    weight_sem,
    halo_send,
    halo_recv,
    ring_send,
    ring_recv,
):
    section_count, band_count, lon_cells, head_width = sizes
    tokens, features = slab.shape
    band_rows = tokens // lon_cells
    half = tokens // 2
    per_group = LANES // head_width
    section = lax.axis_index("section")
    band = lax.axis_index("lat")
    following = lax.rem(section + 1, section_count)
    preceding = lax.rem(section + section_count - 1, section_count)
    has_low = band > 0
    has_high = band < band_count - 1
    shifted = lax.rem(section, 2)

    barrier = pltpu.get_barrier_semaphore()
    pl.semaphore_signal(barrier, inc=1, device_id={"section": following}, device_id_type=MESH)
    pl.semaphore_signal(barrier, inc=1, device_id={"section": preceding}, device_id_type=MESH)

    @pl.when(has_low)
    def _():
        pl.semaphore_signal(barrier, inc=1, device_id={"lat": band - 1}, device_id_type=MESH)

    @pl.when(has_high)
    def _():
        pl.semaphore_signal(barrier, inc=1, device_id={"lat": band + 1}, device_id_type=MESH)

    loads = [
        pltpu.make_async_copy(source, target, weight_sem.at[index])
        for index, (source, target) in enumerate(
            ((in_hbm, w_in), (out_hbm, w_out), (up_hbm, w_up), (down_hbm, w_down))
        )
    ]
    for load in loads:
        load.start()

    offset = offsets[0] * shifted
    key_starts = [half * (1 - shifted), half + half * shifted]
    for side in range(2):
        shape = (half, tokens)
        first_row = band * band_rows - band_rows // 2 + (
            (1 - shifted) * (band_rows // 2) if side == 0 else (1 + shifted) * (band_rows // 2)
        )
        _, query_lon = split_index(lax.broadcasted_iota(jnp.int32, shape, 0), lon_cells, band_rows)
        key_row, key_lon = split_index(lax.broadcasted_iota(jnp.int32, shape, 1), lon_cells, band_rows)
        tiles = []
        for lon in (query_lon, key_lon):
            moved = lon - offset
            moved = jnp.where(moved < 0, moved + lon_cells, moved)
            tiles.append(split_index(moved, WIN_LON, lon_cells // WIN_LON)[0])
        row = key_row + first_row
        inside = (tiles[0] == tiles[1]) & (row >= 0) & (row < band_rows * band_count)
        window[side] = jnp.where(inside, 1.0, 0.0)

    def project(source, target_rows, with_queries):
        def step(index, carry):
            start = pl.multiple_of(index * COLS, COLS)
            columns = pl.ds(start, COLS)
            rows = source[...]
            if with_queries:
                queries[:, columns] = head_unit(dot(rows, w_in[:, columns]), head_width)
            key = head_unit(
                dot(rows, w_in[:, pl.ds(pl.multiple_of(features + start, COLS), COLS)]), head_width
            )
            value = dot(
                rows, w_in[:, pl.ds(pl.multiple_of(2 * features + start, COLS), COLS)]
            ).astype(BF16)
            done = 0
            for first, count in target_rows:
                keys[first : first + count, columns] = key[done : done + count]
                values[first : first + count, columns] = value[done : done + count]
                done += count
            return carry

        lax.fori_loop(0, features // COLS, step, 0)

    def attend(index, carry):
        columns = pl.ds(pl.multiple_of(index * LANES, LANES), LANES)
        lane = lax.broadcasted_iota(jnp.int32, (1, LANES), 1)
        own = [
            jnp.where((lane >= low) & (lane < low + head_width), 1.0, 0.0).astype(BF16)
            for low in range(0, LANES, head_width)
        ]
        taps = [
            [position_kernel[lat, pl.ds(lon, 1), columns] for lon in range(3)]
            for lat in range(WIN_LAT + 1)
        ]
        for side in range(2):
            spots = []
            for row in range(side * band_rows // 2, (side + 1) * band_rows // 2):
                strips = [
                    values[(row + lat) * lon_cells : (row + lat + 1) * lon_cells, columns].astype(F32)
                    for lat in range(WIN_LAT + 1)
                ]
                parts = []
                for lon in range(3):
                    part = taps[0][lon] * strips[0]
                    for lat in range(1, WIN_LAT + 1):
                        part = part + taps[lat][lon] * strips[lat]
                    parts.append(part)
                spots.append(
                    parts[1]
                    + pltpu.roll(parts[0], 1, 0)
                    + pltpu.roll(parts[2], lon_cells - 1, 0)
                )
            total = jnp.concatenate(spots, axis=0)
            near = pl.ds(pl.multiple_of(key_starts[side], half), tokens)
            key = keys[near, columns]
            value = values[near, columns]
            query = queries[side * half : (side + 1) * half, columns]
            for head in range(per_group):
                scores = lax.dot_general(
                    query * own[head], key, (((1,), (1,)), ((), ())), preferred_element_type=F32
                )
                raised = jnp.exp(scores * head_scale[index * per_group + head]) * window[side]
                inverse = 1.0 / jnp.sum(raised, axis=-1, keepdims=True)
                total = total + dot((raised * inverse).astype(BF16), value * own[head])
            blended[side * half : (side + 1) * half, columns] = total.astype(BF16)
        return carry

    def expand(index, carry):
        columns = pl.ds(pl.multiple_of(index * COLS, COLS), COLS)
        wide = dot(normed_mix[...], w_up[:, columns])
        hidden[:, columns] = (wide * 0.5 * (1.0 + lax.erf(wide * math.sqrt(0.5)))).astype(BF16)
        return carry

    def halo_copies(tick):
        up = pltpu.make_async_remote_copy(
            src_ref=normed.at[tick, pl.ds(half, half)],
            dst_ref=halo.at[tick, pl.ds(0, half)],
            send_sem=halo_send.at[tick, 0],
            recv_sem=halo_recv.at[tick, 0],
            device_id={"lat": jnp.minimum(band + 1, band_count - 1)},
            device_id_type=MESH,
        )
        down = pltpu.make_async_remote_copy(
            src_ref=normed.at[tick, pl.ds(0, half)],
            dst_ref=halo.at[tick, pl.ds(half, half)],
            send_sem=halo_send.at[tick, 1],
            recv_sem=halo_recv.at[tick, 1],
            device_id={"lat": jnp.maximum(band - 1, 0)},
            device_id_type=MESH,
        )
        return up, down

    def ring_copy(tick, part):
        columns = pl.ds(part * COLS, COLS)
        return pltpu.make_async_remote_copy(
            src_ref=ring_out.at[tick, :, columns],
            dst_ref=ring_in.at[tick, :, columns],
            send_sem=ring_send.at[tick, part],
            recv_sem=ring_recv.at[tick, part],
            device_id={"section": following},
            device_id_type=MESH,
        )

    parts = features // COLS
    for tick in range(TICKS):
        if tick:
            for part in range(parts):
                ring_copy(tick - 1, part).wait()
        member = lax.rem(section - tick + section_count * TICKS, section_count)
        code = codes[tick, member]
        table_row = lax.broadcasted_iota(jnp.int32, table.shape, 0)
        perturb = jnp.sum(jnp.where(table_row == code, table[...], 0.0), axis=0, keepdims=True)

        def enter(index, carry):
            rows = pl.ds(pl.multiple_of(index * lon_cells, lon_cells), lon_cells)
            current = slab[rows, :] if tick == 0 else ring_in[tick - 1, rows, :].astype(F32)
            current = current + perturb + land[rows, :] * land_embed[...]
            stream[rows, :] = current
            normed[tick, rows, :] = norm_scale(current, attention_gain[...]).astype(BF16)
            return carry

        lax.fori_loop(0, band_rows, enter, 0)

        if tick == 0:
            ends = (band == 0).astype(jnp.int32) + (band == band_count - 1).astype(jnp.int32)
            pl.semaphore_wait(barrier, 4 - ends)

        up, down = halo_copies(tick)

        @pl.when(has_high)
        def _():
            up.start()

        @pl.when(has_low)
        def _():
            down.start()

        @pl.when(jnp.logical_not(has_low))
        def _():
            halo[tick, 0:half, :] = jnp.zeros((half, features), BF16)

        @pl.when(jnp.logical_not(has_high))
        def _():
            halo[tick, half:tokens, :] = jnp.zeros((half, features), BF16)

        if tick == 0:
            loads[0].wait()
        project(normed.at[tick], ((half, tokens),), True)

        @pl.when(has_high)
        def _():
            up.wait_send()
            down.wait_recv()

        @pl.when(has_low)
        def _():
            down.wait_send()
            up.wait_recv()

        project(halo.at[tick], ((0, half), (half + tokens, half)), False)
        lax.fori_loop(0, features // LANES, attend, 0)

        if tick == 0:
            loads[1].wait()
        for part in range(parts):
            columns = slice(part * COLS, (part + 1) * COLS)
            mixed[:, columns] = stream[:, columns] + dot(blended[...], w_out[:, columns])

        def middle(index, carry):
            rows = pl.ds(pl.multiple_of(index * lon_cells, lon_cells), lon_cells)
            normed_mix[rows, :] = norm_scale(mixed[rows, :], feed_gain[...]).astype(BF16)
            return carry

        lax.fori_loop(0, band_rows, middle, 0)
        if tick == 0:
            loads[2].wait()
        lax.fori_loop(0, w_up.shape[1] // COLS, expand, 0)
        if tick == 0:
            loads[3].wait()
        for part in range(parts):
            columns = slice(part * COLS, (part + 1) * COLS)
            finished = mixed[:, columns] + dot(hidden[...], w_down[:, columns])
            if tick + 1 < TICKS:
                ring_out[tick, :, columns] = finished.astype(BF16)
                ring_copy(tick, part).start()
            else:
                result[:, columns] = finished


def solution(mesh):
    section_count = mesh.shape["section"]
    band_count = mesh.shape["lat"]

    def body(
        member_slabs,
        member_codes,
        member_table,
        land_sea,
        land_embed,
        attention_gain,
        project_in,
        logit_scale,
        position_kernel,
        project_out,
        feed_gain,
        expand_weight,
        reduce_weight,
        window_offset,
    ):
        _, band_rows, lon_cells, features = member_slabs.shape
        assert band_rows == WIN_LAT
        tokens = band_rows * lon_cells
        hidden_width = expand_weight.shape[2]
        head_width = features // logit_scale.shape[1]
        parts = features // COLS
        links = max(TICKS - 1, 1)
        smem = pl.BlockSpec(memory_space=pltpu.SMEM)
        vmem = pl.BlockSpec(memory_space=pltpu.VMEM)
        hbm = pl.BlockSpec(memory_space=pl.ANY)
        updated = pl.pallas_call(
            functools.partial(kernel, (section_count, band_count, lon_cells, head_width)),
            out_shape=jax.ShapeDtypeStruct((tokens, features), F32),
            in_specs=[smem] * 3 + [vmem] * 7 + [hbm] * 4,
            out_specs=vmem,
            scratch_shapes=[
                pltpu.VMEM((features, 3 * features), BF16),
                pltpu.VMEM((features, features), BF16),
                pltpu.VMEM((features, hidden_width), BF16),
                pltpu.VMEM((hidden_width, features), BF16),
                pltpu.VMEM((tokens, features), F32),
                pltpu.VMEM((tokens, features), F32),
                pltpu.VMEM((TICKS, tokens, features), BF16),
                pltpu.VMEM((TICKS, tokens, features), BF16),
                pltpu.VMEM((tokens, features), BF16),
                pltpu.VMEM((2 * tokens, features), BF16),
                pltpu.VMEM((2 * tokens, features), BF16),
                pltpu.VMEM((tokens, features), BF16),
                pltpu.VMEM((tokens, features), BF16),
                pltpu.VMEM((tokens, hidden_width), BF16),
                pltpu.VMEM((2, tokens // 2, tokens), F32),
                pltpu.VMEM((links, tokens, features), BF16),
                pltpu.VMEM((links, tokens, features), BF16),
                pltpu.SemaphoreType.DMA((4,)),
                pltpu.SemaphoreType.DMA((TICKS, 2)),
                pltpu.SemaphoreType.DMA((TICKS, 2)),
                pltpu.SemaphoreType.DMA((links, parts)),
                pltpu.SemaphoreType.DMA((links, parts)),
            ],
            compiler_params=pltpu.CompilerParams(
                collective_id=0, has_side_effects=True, vmem_limit_bytes=60 * 1024 * 1024
            ),
        )(
            member_codes,
            window_offset,
            logit_scale[0],
            member_slabs.reshape(tokens, features),
            member_table,
            land_sea.astype(F32).reshape(tokens, 1),
            land_embed,
            attention_gain,
            feed_gain,
            position_kernel[0],
            project_in[0],
            project_out[0],
            expand_weight[0],
            reduce_weight[0],
        )
        return updated.reshape(member_slabs.shape)

    placed = (
        P(("groups", "section"), "lat", None, None),
        P(None, "groups"),
        P(),
        P("lat", None),
        P("section", None),
        P("section", None),
        P("section", None, None),
        P("section", None),
        P("section", None, None, None),
        P("section", None, None),
        P("section", None),
        P("section", None, None),
        P("section", None, None),
        P("section"),
    )
    return jax.shard_map(
        body,
        mesh=mesh,
        in_specs=placed,
        out_specs=P(("groups", "section"), "lat", None, None),
        check_vma=False,
    )
```

profile of v0, /device:TPU:0, one launch (start us, length us, event | category | flops | bytes accessed | tf_op | source)
XLA Modules:
  0.0 49.0 jit_solution(15629749542453553476)
XLA Ops:
  0.7 0.7 %convert_element_type.3 = f32[4,64]{1,0:T(4,128)S(1)} convert(s32[4,64]{1,0:T(4,128)} %param.17) | non-fusion elementwise | flops 256 | bytes 2048 | tf_op jit(solution)/shard_map/convert_element_type | solution.py:403
  1.3 1.4 %copy.18 = f32[1,5,3,768]{3,2,0,1:T(4,128)} copy(f32[1,5,3,768]{3,0,2,1:T(1,128)} %param.22) | data formatting | bytes 92160
  2.8 0.8 %reshape.12.land = f32[256,1]{1,0:T(8,128)} reshape(f32[4,64]{1,0:T(4,128)S(1)} %convert_element_type.3) | data formatting | bytes 2048 | tf_op jit(solution)/shard_map/reshape | solution.py:403
  3.6 43.4 %shard_map.136 = f32[256,768]{1,0:T(8,128)} custom-call(s32[2,4]{1,0:T(2,128)} %codes.1, s32[1]{0:T(128)S(6)} %copy.20.offsets, f32[12]{0:T(128)} %bitcast.17, f32[256,768]{1,0:T(8,128)} %bitcast.15, f32[32,768]{1,0:T(8,128)} %table.1, f32[256,1]{1,0:T(8,128)} %reshape.12.land, f32[1,768]{1,0:T(1,128)} %land_embed.1, f32[1,768]{1,0:T(1,128)} %attention_gain.1, ...), custom_call_target="tpu_custom_call" | custom-call | tf_op jit(solution)/shard_map/pallas_call | solution.py:365
  46.9 2.1 %copy.21 = f32[1,4,64,768]{3,2,1,0:T(8,128)} copy(f32[1,4,64,768]{3,2,1,0:T(8,128)} %bitcast.13) | data formatting | bytes 1572864
where the time goes:
time: 49.3 us; the launch traced here: 49 us
  Pallas kernels  43.4 us (88%)
  local copies, waits for them, and re-layouts  4.3 us (9%)
  other arithmetic  0.68 us (1%)
  between operations  0.66 us (1%)
    pallas_call x1, Pallas kernels, body(): pl.pallas_call(functools.partial(kernel, (section_count, band_count, lon_...  43.4 us
    unnamed x2, local copies, waits for them, and re-layouts  3.51 us

commit v1 on v0

--- a/solution.py
+++ b/solution.py
@@ -84,6 +84,7 @@
     normed_mix,
     hidden,
     window,
+    land_column,
     ring_out,
     ring_in,
     weight_sem,
@@ -123,8 +124,15 @@
             ((in_hbm, w_in), (out_hbm, w_out), (up_hbm, w_up), (down_hbm, w_down))
         )
     ]
-    for load in loads:
-        load.start()
+    loads[0].start()
+
+    square = (lon_cells, lon_cells)
+    diagonal = lax.broadcasted_iota(jnp.int32, square, 0) == lax.broadcasted_iota(jnp.int32, square, 1)
+    for row in range(band_rows):
+        marks = jnp.broadcast_to(land[row : row + 1, :].astype(F32), square)
+        land_column[row * lon_cells : (row + 1) * lon_cells, :] = jnp.sum(
+            jnp.where(diagonal, marks, 0.0), axis=-1, keepdims=True
+        )
 
     offset = offsets[0] * shifted
     key_starts = [half * (1 - shifted), half + half * shifted]
@@ -146,16 +154,16 @@
 
     def project(source, target_rows, with_queries):
         def step(index, carry):
-            start = pl.multiple_of(index * COLS, COLS)
+            start = index * COLS
             columns = pl.ds(start, COLS)
             rows = source[...]
             if with_queries:
                 queries[:, columns] = head_unit(dot(rows, w_in[:, columns]), head_width)
             key = head_unit(
-                dot(rows, w_in[:, pl.ds(pl.multiple_of(features + start, COLS), COLS)]), head_width
+                dot(rows, w_in[:, pl.ds(features + start, COLS)]), head_width
             )
             value = dot(
-                rows, w_in[:, pl.ds(pl.multiple_of(2 * features + start, COLS), COLS)]
+                rows, w_in[:, pl.ds(2 * features + start, COLS)]
             ).astype(BF16)
             done = 0
             for first, count in target_rows:
@@ -164,17 +172,18 @@
                 done += count
             return carry
 
-        lax.fori_loop(0, features // COLS, step, 0)
+        for index in range(features // COLS):
+            step(index, 0)
 
     def attend(index, carry):
-        columns = pl.ds(pl.multiple_of(index * LANES, LANES), LANES)
+        columns = pl.ds(index * LANES, LANES)
         lane = lax.broadcasted_iota(jnp.int32, (1, LANES), 1)
         own = [
             jnp.where((lane >= low) & (lane < low + head_width), 1.0, 0.0).astype(BF16)
             for low in range(0, LANES, head_width)
         ]
         taps = [
-            [position_kernel[lat, pl.ds(lon, 1), columns] for lon in range(3)]
+            [position_kernel[lat * 3 + lon, :, columns] for lon in range(3)]
             for lat in range(WIN_LAT + 1)
         ]
         for side in range(2):
@@ -200,18 +209,30 @@
             key = keys[near, columns]
             value = values[near, columns]
             query = queries[side * half : (side + 1) * half, columns]
+            scores = lax.dot_general(
+                jnp.concatenate([query * mark for mark in own], axis=0),
+                key,
+                (((1,), (1,)), ((), ())),
+                preferred_element_type=F32,
+            )
+            weights = []
             for head in range(per_group):
-                scores = lax.dot_general(
-                    query * own[head], key, (((1,), (1,)), ((), ())), preferred_element_type=F32
+                mine = scores[head * half : (head + 1) * half]
+                raised = jnp.exp(mine * head_scale[index * per_group + head]) * window[side]
+                inverse = 1.0 / jnp.sum(raised, axis=-1, keepdims=True)
+                weights.append((raised * inverse).astype(BF16))
+            found = dot(jnp.concatenate(weights, axis=0), value)
+            attended = found[:half]
+            for head in range(1, per_group):
+                attended = jnp.where(
+                    lane >= head * head_width, found[head * half : (head + 1) * half], attended
                 )
-                raised = jnp.exp(scores * head_scale[index * per_group + head]) * window[side]
-                inverse = 1.0 / jnp.sum(raised, axis=-1, keepdims=True)
-                total = total + dot((raised * inverse).astype(BF16), value * own[head])
+            total = total + attended
             blended[side * half : (side + 1) * half, columns] = total.astype(BF16)
         return carry
 
     def expand(index, carry):
-        columns = pl.ds(pl.multiple_of(index * COLS, COLS), COLS)
+        columns = pl.ds(index * COLS, COLS)
         wide = dot(normed_mix[...], w_up[:, columns])
         hidden[:, columns] = (wide * 0.5 * (1.0 + lax.erf(wide * math.sqrt(0.5)))).astype(BF16)
         return carry
@@ -259,7 +280,7 @@
         def enter(index, carry):
             rows = pl.ds(pl.multiple_of(index * lon_cells, lon_cells), lon_cells)
             current = slab[rows, :] if tick == 0 else ring_in[tick - 1, rows, :].astype(F32)
-            current = current + perturb + land[rows, :] * land_embed[...]
+            current = current + perturb + land_column[rows, :] * land_embed[...]
             stream[rows, :] = current
             normed[tick, rows, :] = norm_scale(current, attention_gain[...]).astype(BF16)
             return carry
@@ -290,6 +311,8 @@
 
         if tick == 0:
             loads[0].wait()
+            for load in loads[1:]:
+                load.start()
         project(normed.at[tick], ((half, tokens),), True)
 
         @pl.when(has_high)
@@ -303,7 +326,8 @@
             up.wait_recv()
 
         project(halo.at[tick], ((0, half), (half + tokens, half)), False)
-        lax.fori_loop(0, features // LANES, attend, 0)
+        for index in range(features // LANES):
+            attend(index, 0)
 
         if tick == 0:
             loads[1].wait()
@@ -319,7 +343,8 @@
         lax.fori_loop(0, band_rows, middle, 0)
         if tick == 0:
             loads[2].wait()
-        lax.fori_loop(0, w_up.shape[1] // COLS, expand, 0)
+        for index in range(w_up.shape[1] // COLS):
+            expand(index, 0)
         if tick == 0:
             loads[3].wait()
         for part in range(parts):
@@ -383,6 +408,7 @@
                 pltpu.VMEM((tokens, features), BF16),
                 pltpu.VMEM((tokens, hidden_width), BF16),
                 pltpu.VMEM((2, tokens // 2, tokens), F32),
+                pltpu.VMEM((tokens, 1), F32),
                 pltpu.VMEM((links, tokens, features), BF16),
                 pltpu.VMEM((links, tokens, features), BF16),
                 pltpu.SemaphoreType.DMA((4,)),
@@ -400,11 +426,11 @@
             logit_scale[0],
             member_slabs.reshape(tokens, features),
             member_table,
-            land_sea.astype(F32).reshape(tokens, 1),
+            land_sea,
             land_embed,
             attention_gain,
             feed_gain,
-            position_kernel[0],
+            position_kernel.reshape(-1, 1, features),
             project_in[0],
             project_out[0],
             expand_weight[0],

time: 49.3 us -> 37.8 us (0.77)
  Pallas kernels: 43.4 us -> 34.8 us
  local copies, waits for them, and re-layouts: 4.3 us -> 2.09 us
  other arithmetic: 0.68 us -> 0 us
    pallas_call x1, Pallas kernels: 43.4 us -> 34.8 us  [body(): pl.pallas_call(functools.partial(kernel, (section_count, band_count, lon_...]
    unnamed x2 -> x1, local copies, waits for them, and re-layouts: 3.51 us -> 2.09 us
    reshape x1 -> x0, local copies, waits for them, and re-layouts: 0.79 us -> none  [body(): land_sea.astype(F32).reshape(tokens, 1)]
    convert_element_type x1 -> x0, other arithmetic: 0.68 us -> none  [body(): land_sea.astype(F32).reshape(tokens, 1)]
where the time goes in v1:
time: 37.8 us; the launch traced here: 37.6 us
  Pallas kernels  34.8 us (92%)
  local copies, waits for them, and re-layouts  2.09 us (6%)
  between operations  0.66 us (2%)
    pallas_call x1, Pallas kernels, body(): pl.pallas_call(functools.partial(kernel, (section_count, band_count, lon_...  34.8 us
    unnamed x1, local copies, waits for them, and re-layouts  2.09 us

profile of v1, /device:TPU:0, one launch (start us, length us, event | category | flops | bytes accessed | tf_op | source)
XLA Modules:
  0.0 37.6 jit_solution(10460140480162016486)
XLA Ops:
  0.7 34.8 %shard_map.136 = f32[256,768]{1,0:T(8,128)} custom-call(s32[2,4]{1,0:T(2,128)} %codes.1, s32[1]{0:T(128)S(6)} %copy.16.offsets, f32[12]{0:T(128)} %bitcast.15, f32[256,768]{1,0:T(8,128)} %bitcast.13, f32[32,768]{1,0:T(8,128)} %table.1, s32[4,64]{1,0:T(4,128)} %land.1, f32[1,768]{1,0:T(1,128)} %land_embed.1, f32[1,768]{1,0:T(1,128)} %attention_gain.1, ...), custom_call_target="tpu_custom_call" | custom-call | tf_op jit(solution)/shard_map/pallas_call | solution.py:390
  35.5 2.1 %copy.17 = f32[1,4,64,768]{3,2,1,0:T(8,128)} copy(f32[1,4,64,768]{3,2,1,0:T(8,128)} %bitcast.9) | data formatting | bytes 1572864

commit v2 on v1

--- a/solution.py
+++ b/solution.py
@@ -121,10 +121,20 @@
     loads = [
         pltpu.make_async_copy(source, target, weight_sem.at[index])
         for index, (source, target) in enumerate(
-            ((in_hbm, w_in), (out_hbm, w_out), (up_hbm, w_up), (down_hbm, w_down))
+            ((out_hbm, w_out), (up_hbm, w_up), (down_hbm, w_down))
         )
     ]
-    loads[0].start()
+    in_loads = []
+    for start in range(0, features, COLS):
+        for base in range(0, 3 * features, features):
+            columns = pl.ds(base + start, COLS)
+            in_loads.append(
+                pltpu.make_async_copy(
+                    in_hbm.at[:, columns], w_in.at[:, columns], weight_sem.at[3 + len(in_loads)]
+                )
+            )
+    for load in in_loads:
+        load.start()
 
     square = (lon_cells, lon_cells)
     diagonal = lax.broadcasted_iota(jnp.int32, square, 0) == lax.broadcasted_iota(jnp.int32, square, 1)
@@ -152,8 +162,11 @@
         inside = (tiles[0] == tiles[1]) & (row >= 0) & (row < band_rows * band_count)
         window[side] = jnp.where(inside, 1.0, 0.0)
 
-    def project(source, target_rows, with_queries):
+    def project(source, target_rows, with_queries, loading):
         def step(index, carry):
+            if loading:
+                for load in in_loads[3 * index : 3 * index + 3]:
+                    load.wait()
             start = index * COLS
             columns = pl.ds(start, COLS)
             rows = source[...]
@@ -278,14 +291,15 @@
         perturb = jnp.sum(jnp.where(table_row == code, table[...], 0.0), axis=0, keepdims=True)
 
         def enter(index, carry):
-            rows = pl.ds(pl.multiple_of(index * lon_cells, lon_cells), lon_cells)
+            rows = pl.ds(index * lon_cells, lon_cells)
             current = slab[rows, :] if tick == 0 else ring_in[tick - 1, rows, :].astype(F32)
             current = current + perturb + land_column[rows, :] * land_embed[...]
             stream[rows, :] = current
             normed[tick, rows, :] = norm_scale(current, attention_gain[...]).astype(BF16)
             return carry
 
-        lax.fori_loop(0, band_rows, enter, 0)
+        for index in range(band_rows):
+            enter(index, 0)
 
         if tick == 0:
             ends = (band == 0).astype(jnp.int32) + (band == band_count - 1).astype(jnp.int32)
@@ -310,10 +324,9 @@
             halo[tick, half:tokens, :] = jnp.zeros((half, features), BF16)
 
         if tick == 0:
-            loads[0].wait()
-            for load in loads[1:]:
+            for load in loads:
                 load.start()
-        project(normed.at[tick], ((half, tokens),), True)
+        project(normed.at[tick], ((half, tokens),), True, tick == 0)
 
         @pl.when(has_high)
         def _():
@@ -325,28 +338,29 @@
             down.wait_send()
             up.wait_recv()
 
-        project(halo.at[tick], ((0, half), (half + tokens, half)), False)
+        project(halo.at[tick], ((0, half), (half + tokens, half)), False, False)
         for index in range(features // LANES):
             attend(index, 0)
 
         if tick == 0:
-            loads[1].wait()
+            loads[0].wait()
         for part in range(parts):
             columns = slice(part * COLS, (part + 1) * COLS)
             mixed[:, columns] = stream[:, columns] + dot(blended[...], w_out[:, columns])
 
         def middle(index, carry):
-            rows = pl.ds(pl.multiple_of(index * lon_cells, lon_cells), lon_cells)
+            rows = pl.ds(index * lon_cells, lon_cells)
             normed_mix[rows, :] = norm_scale(mixed[rows, :], feed_gain[...]).astype(BF16)
             return carry
 
-        lax.fori_loop(0, band_rows, middle, 0)
+        for index in range(band_rows):
+            middle(index, 0)
         if tick == 0:
-            loads[2].wait()
+            loads[1].wait()
         for index in range(w_up.shape[1] // COLS):
             expand(index, 0)
         if tick == 0:
-            loads[3].wait()
+            loads[2].wait()
         for part in range(parts):
             columns = slice(part * COLS, (part + 1) * COLS)
             finished = mixed[:, columns] + dot(hidden[...], w_down[:, columns])
@@ -411,7 +425,7 @@
                 pltpu.VMEM((tokens, 1), F32),
                 pltpu.VMEM((links, tokens, features), BF16),
                 pltpu.VMEM((links, tokens, features), BF16),
-                pltpu.SemaphoreType.DMA((4,)),
+                pltpu.SemaphoreType.DMA((3 + 3 * parts,)),
                 pltpu.SemaphoreType.DMA((TICKS, 2)),
                 pltpu.SemaphoreType.DMA((TICKS, 2)),
                 pltpu.SemaphoreType.DMA((links, parts)),

time: 37.8 us -> 36.6 us (0.968)
  Pallas kernels: 34.8 us -> 33.7 us
    pallas_call x1, Pallas kernels: 34.8 us -> 33.7 us  [body(): pl.pallas_call(functools.partial(kernel, (section_count, band_count, lon_...]
where the time goes in v2:
time: 36.6 us; the launch traced here: 36.4 us
  Pallas kernels  33.7 us (92%)
  local copies, waits for them, and re-layouts  2.09 us (6%)
  between operations  0.66 us (2%)
    pallas_call x1, Pallas kernels, body(): pl.pallas_call(functools.partial(kernel, (section_count, band_count, lon_...  33.7 us
    unnamed x1, local copies, waits for them, and re-layouts  2.09 us

profile of v2, /device:TPU:0, one launch (start us, length us, event | category | flops | bytes accessed | tf_op | source)
XLA Modules:
  0.0 36.4 jit_solution(2870661297490310167)
XLA Ops:
  0.7 33.7 %shard_map.136 = f32[256,768]{1,0:T(8,128)} custom-call(s32[2,4]{1,0:T(2,128)} %codes.1, s32[1]{0:T(128)S(6)} %copy.16.offsets, f32[12]{0:T(128)} %bitcast.15, f32[256,768]{1,0:T(8,128)} %bitcast.13, f32[32,768]{1,0:T(8,128)} %table.1, s32[4,64]{1,0:T(4,128)} %land.1, f32[1,768]{1,0:T(1,128)} %land_embed.1, f32[1,768]{1,0:T(1,128)} %attention_gain.1, ...), custom_call_target="tpu_custom_call" | custom-call | tf_op jit(solution)/shard_map/pallas_call | solution.py:404
  34.3 2.1 %copy.17 = f32[1,4,64,768]{3,2,1,0:T(8,128)} copy(f32[1,4,64,768]{3,2,1,0:T(8,128)} %bitcast.9) | data formatting | bytes 1572864
